TPU v7x, 512 devices: a whole 4x4x16 slice. The times are simulated.
512 devices in a mesh: blk: 32 (over z, x_hi), bfly: 16 (over y, x_lo, core).
Axes of the slice: x: 4 (x_hi: 2, x_lo: 2; x = x_hi * 2 + x_lo), y: 4, z: 16, core: 2. Of those that a mesh axis runs over, the one named last changes fastest.
Arguments:
- port_vectors: bfloat16 [32, 16, 768, 128], P('blk', 'bfly'), may hold values from -6 to 6
- column_leaf: bfloat16 [32, 16, 384, 768], P('blk', 'bfly'), may hold values from -0.21875 to 0.21875
- transfer: bfloat16 [32, 4, 16, 384, 768], P('blk', None, 'bfly'), may hold values from -0.21875 to 0.21875
- row_leaf: bfloat16 [32, 16, 768, 384], P('blk', 'bfly'), may hold values from -0.3125 to 0.3125
Outputs:
- field: bfloat16 [16, 768, 128], P('bfly', 'blk')
All inputs are finite; a program needn't handle non-finite values.
Results may differ from a plain program's by a relative error of at most 0.0095.
Values may be sent and summed in bfloat16 or wider, within the bound.
No kernel may reach another device: no remote copies, remote signals or barrier semaphores. Data moves between devices by JAX's collectives and lax.ppermute only.
A program may use at most 64 MiB of HBM per device.

v0:
```python
import math

import jax
import jax.numpy as jnp
from jax import lax
from jax.sharding import PartitionSpec as P


def from_partner(array, axis, bit):
    return lax.ppermute(array, axis, [(i, i ^ 1 << bit) for i in range(lax.axis_size(axis))])


def cut_along(array, dim, count):
    before, after = (array.shape[:dim], array.shape[dim + 1 :])
    return jnp.moveaxis(array.reshape(*before, count, -1, *after), dim, 0)


def sent_and_summed(array, axis, dim):
    count = lax.axis_size(axis)
    tiles = lax.all_to_all(cut_along(array, dim, count), axis, 0, 0, tiled=True)
    return jnp.sum(tiles, axis=0)


def local(port_vectors, column_leaf, transfer, row_leaf):
    rank_rows = column_leaf.shape[2]
    bit_count = lax.axis_size("bfly").bit_length() - 1
    position = lax.axis_index("bfly")
    state = jnp.dot(
        column_leaf[0, 0], port_vectors[0, 0], preferred_element_type=jnp.float32
    ).astype(jnp.bfloat16)
    for level in range(transfer.shape[1]):
        bit = level % bit_count
        partner_state = from_partner(state, "bfly", bit)
        mine_low = position // 2**bit % 2 == 0
        lower = jnp.where(mine_low, state, partner_state)
        upper = jnp.where(mine_low, partner_state, state)
        matrix = transfer[0, level, 0]
        mixed = jnp.dot(matrix[:, :rank_rows], lower, preferred_element_type=jnp.float32)
        mixed = mixed + jnp.dot(matrix[:, rank_rows:], upper, preferred_element_type=jnp.float32)
        state = mixed.astype(jnp.bfloat16)
    leaf_rows = row_leaf[0, 0]
    owned = leaf_rows.shape[0] // lax.axis_size("blk")
    partial_rows = jnp.dot(leaf_rows, state, preferred_element_type=jnp.float32)
    summed = sent_and_summed(partial_rows, "blk", 0)
    scaled = summed * (1.0 / math.sqrt(lax.axis_size("blk")))
    return scaled.astype(jnp.bfloat16).reshape(1, owned, scaled.shape[1])


def solution(mesh):
    placed = (
        P("blk", "bfly", None, None),
        P("blk", "bfly", None, None),
        P("blk", None, "bfly", None, None),
        P("blk", "bfly", None, None),
    )
    return jax.shard_map(
        local, mesh=mesh, in_specs=placed, out_specs=P("bfly", "blk", None), check_vma=False
    )
```

profile of v0, /device:TPU:24, one launch (start us, length us, event | category | flops | bytes accessed | tf_op | source)
XLA Modules:
  0.0 72.7 jit_solution(13213902842206353997)
XLA Ops:
  0.0 0.0 copy-start
  0.0 1.5 %convolution_convert_fusion = bf16[384,128]{1,0:T(8,128)(2,1)S(1)} fusion(bf16[1,1,384,768]{3,2,1,0:T(8,128)(2,1)} %param.5, bf16[1,1,768,128]{3,2,1,0:T(8,128)(2,1)} %param.4), kind=kOutput, calls=%fused_computation.9 | convolution fusion | flops 75546624 | bytes 884736 | tf_op jit(solution)/shard_map/dot_general | solution.py:28
  1.5 1.9 %collective-permute-start = (bf16[384,128]{1,0:T(8,128)(2,1)S(1)}, bf16[384,128]{1,0:T(8,128)(2,1)S(1)}, u32[]{:S(2)}, u32[]{:S(2)}) collective-permute-start(bf16[384,128]{1,0:T(8,128)(2,1)S(1)} %convolution_convert_fusion), channel_id=1, source_target_pairs={{0,1},{1,0},{2,3},{3,2},{4,5},{5,4},{6,7},{7,6},{8,9},{9,8},{10,11... | collective-permute-start | bytes 294920 | tf_op jit(solution)/shard_map/ppermute | solution.py:10
  3.4 1.8 %slice_bitcast_fusion.3 = (bf16[384,768]{1,0:T(8,128)(2,1)S(1)}, bf16[384,768]{1,0:T(8,128)(2,1)S(1)}, bf16[384,768]{1,0:T(8,128)(2,1)S(1)}, bf16[384,768]{1,0:T(8,128)(2,1)S(1)}) fusion(bf16[1,4,1,384,768]{4,3,2,1,0:T(8,128)(2,1)} %param.6), kind=kLoop, calls=%fused_computation.18 | loop fusion | bytes 4718592 | tf_op jit(solution)/shard_map/squeeze | solution.py:37
  5.2 0.0 collective-permute-done
  5.2 0.3 fusion.19
  5.5 0.3 fusion.6
  5.7 3.4 %collective-permute-start.1 = (bf16[384,128]{0,1:T(8,128)(2,1)S(1)}, bf16[384,128]{0,1:T(8,128)(2,1)S(1)}, u32[]{:S(2)}, u32[]{:S(2)}) collective-permute-start(bf16[384,128]{0,1:T(8,128)(2,1)S(1)} %fusion.6), channel_id=1, source_target_pairs={{0,2},{1,3},{2,0},{3,1},{4,6},{5,7},{6,4},{7,5},{8,10},{9,11},{10,... | collective-permute-start | bytes 294920 | tf_op jit(solution)/shard_map/ppermute | solution.py:10
  9.2 3.7 %collective-permute-done.1 = bf16[384,128]{0,1:T(8,128)(2,1)S(1)} collective-permute-done((bf16[384,128]{0,1:T(8,128)(2,1)S(1)}, bf16[384,128]{0,1:T(8,128)(2,1)S(1)}, u32[]{:S(2)}, u32[]{:S(2)}) %collective-permute-start.1) | collective-permute-done | bytes 98336 | tf_op jit(solution)/shard_map/ppermute | solution.py:10
  12.8 0.2 fusion.16
  13.1 0.2 fusion.5
  13.3 2.7 %collective-permute-start.2 = (bf16[384,128]{0,1:T(8,128)(2,1)S(1)}, bf16[384,128]{0,1:T(8,128)(2,1)S(1)}, u32[]{:S(2)}, u32[]{:S(2)}) collective-permute-start(bf16[384,128]{0,1:T(8,128)(2,1)S(1)} %fusion.5), channel_id=1, source_target_pairs={{0,4},{1,5},{2,6},{3,7},{4,0},{5,1},{6,2},{7,3},{8,12},{9,13},{10,... | collective-permute-start | bytes 294920 | tf_op jit(solution)/shard_map/ppermute | solution.py:10
  16.0 3.8 %collective-permute-done.2 = bf16[384,128]{0,1:T(8,128)(2,1)S(1)} collective-permute-done((bf16[384,128]{0,1:T(8,128)(2,1)S(1)}, bf16[384,128]{0,1:T(8,128)(2,1)S(1)}, u32[]{:S(2)}, u32[]{:S(2)}) %collective-permute-start.2) | collective-permute-done | bytes 98336 | tf_op jit(solution)/shard_map/ppermute | solution.py:10
  19.8 0.2 fusion.13
  20.0 0.2 fusion.4
  20.3 7.0 %collective-permute-start.3 = (bf16[384,128]{0,1:T(8,128)(2,1)S(1)}, bf16[384,128]{0,1:T(8,128)(2,1)S(1)}, u32[]{:S(2)}, u32[]{:S(2)}) collective-permute-start(bf16[384,128]{0,1:T(8,128)(2,1)S(1)} %fusion.4), channel_id=1, source_target_pairs={{0,8},{1,9},{2,10},{3,11},{4,12},{5,13},{6,14},{7,15},{8,0},{9,1},... | collective-permute-start | bytes 294920 | tf_op jit(solution)/shard_map/ppermute | solution.py:10
  27.3 2.5 %collective-permute-done.3 = bf16[384,128]{0,1:T(8,128)(2,1)S(1)} collective-permute-done((bf16[384,128]{0,1:T(8,128)(2,1)S(1)}, bf16[384,128]{0,1:T(8,128)(2,1)S(1)}, u32[]{:S(2)}, u32[]{:S(2)}) %collective-permute-start.3) | collective-permute-done | bytes 98336 | tf_op jit(solution)/shard_map/ppermute | solution.py:10
  29.9 0.2 fusion.9
  30.1 0.0 copy-done
  30.1 0.5 convolution_bitcast_fusion
  30.7 0.2 copy.5
  30.9 41.2 %all_to_all.5 = f32[32,24,128]{2,1,0:T(8,128)S(1)} all-to-all(f32[32,24,128]{2,1,0:T(8,128)S(1)} %bitcast.28), channel_id=1, replica_groups=mesh['blk'=32,'bfly'=16] {'blk'}, dimensions={0} | all-to-all | bytes 786432 | tf_op jit(solution)/shard_map/all_to_all | solution.py:20
  72.1 0.6 fusion.41
  (1 shorter events, 0.0 us)
Async XLA Ops:
  0.0 30.1 %copy-start = (bf16[1,1,768,384]{3,2,1,0:T(8,128)(2,1)S(1)}, bf16[1,1,768,384]{3,2,1,0:T(8,128)(2,1)}, u32[]{:S(2)}) copy-start(bf16[1,1,768,384]{3,2,1,0:T(8,128)(2,1)} %param.7) | copy-start | bytes 1769476
  1.5 3.7 %collective-permute-start = (bf16[384,128]{1,0:T(8,128)(2,1)S(1)}, bf16[384,128]{1,0:T(8,128)(2,1)S(1)}, u32[]{:S(2)}, u32[]{:S(2)}) collective-permute-start(bf16[384,128]{1,0:T(8,128)(2,1)S(1)} %convolution_convert_fusion), channel_id=1, source_target_pairs={{0,1},{1,0},{2,3},{3,2},{4,5},{5,4},{6,7},{7,6},{8,9},{9,8},{10,11... | collective-permute-start | bytes 294920 | tf_op jit(solution)/shard_map/ppermute | solution.py:10
  5.7 7.1 %collective-permute-start.1 = (bf16[384,128]{0,1:T(8,128)(2,1)S(1)}, bf16[384,128]{0,1:T(8,128)(2,1)S(1)}, u32[]{:S(2)}, u32[]{:S(2)}) collective-permute-start(bf16[384,128]{0,1:T(8,128)(2,1)S(1)} %fusion.6), channel_id=1, source_target_pairs={{0,2},{1,3},{2,0},{3,1},{4,6},{5,7},{6,4},{7,5},{8,10},{9,11},{10,... | collective-permute-start | bytes 294920 | tf_op jit(solution)/shard_map/ppermute | solution.py:10
  13.3 6.5 %collective-permute-start.2 = (bf16[384,128]{0,1:T(8,128)(2,1)S(1)}, bf16[384,128]{0,1:T(8,128)(2,1)S(1)}, u32[]{:S(2)}, u32[]{:S(2)}) collective-permute-start(bf16[384,128]{0,1:T(8,128)(2,1)S(1)} %fusion.5), channel_id=1, source_target_pairs={{0,4},{1,5},{2,6},{3,7},{4,0},{5,1},{6,2},{7,3},{8,12},{9,13},{10,... | collective-permute-start | bytes 294920 | tf_op jit(solution)/shard_map/ppermute | solution.py:10
  20.3 9.6 %collective-permute-start.3 = (bf16[384,128]{0,1:T(8,128)(2,1)S(1)}, bf16[384,128]{0,1:T(8,128)(2,1)S(1)}, u32[]{:S(2)}, u32[]{:S(2)}) collective-permute-start(bf16[384,128]{0,1:T(8,128)(2,1)S(1)} %fusion.4), channel_id=1, source_target_pairs={{0,8},{1,9},{2,10},{3,11},{4,12},{5,13},{6,14},{7,15},{8,0},{9,1},... | collective-permute-start | bytes 294920 | tf_op jit(solution)/shard_map/ppermute | solution.py:10
where the time goes:
time: 72.9 us; the launch traced here: 72.7 us
  blocking collectives  41.2 us (57%)
  starting transfers between devices  15 us (21%)
  waiting for transfers between devices  10 us (14%)
  matrix products  3.68 us (5%)
  local copies, waits for them, and re-layouts  1.92 us (3%)
    all_to_all x1, blocking collectives, sent_and_summed(): tiles = lax.all_to_all(cut_along(array, dim, count), axis, 0, 0, tiled=True)  41.2 us
    ppermute x4, starting transfers between devices, from_partner(): lax.ppermute(array, axis, [(i, i ^ 1 << bit) for i in range(lax.axis_size...  15 us
    ppermute x4, waiting for transfers between devices, from_partner(): lax.ppermute(array, axis, [(i, i ^ 1 << bit) for i in range(lax.axis_size...  10 us
    squeeze x1, local copies, waits for them, and re-layouts, local(): matrix = transfer[0, level, 0]  1.76 us
    dot_general x1, matrix products, local(): jnp.dot(column_leaf[0, 0], port_vectors[0, 0], preferred_element_type=jnp...  1.48 us
  transfers between devices with their start and end apart: 4, of which 3 were waited for; matrix products, arithmetic and copies ran while one was open for 2% of the time, Pallas kernels for 0%

commit v1 on v0

v1 whole, which is shorter than its diff:
```python
import math

import jax
import jax.numpy as jnp
from jax import lax
from jax.sharding import PartitionSpec as P


def with_partner(array, axis, bit):
    pairs = [[i, i | 1 << bit] for i in range(lax.axis_size(axis)) if not i >> bit & 1]
    return lax.all_gather(array, axis, axis_index_groups=pairs, tiled=True)


def sent_and_summed(array, axis):
    count = lax.axis_size(axis)
    tiles = array.reshape(count, -1, array.shape[1])
    tiles = lax.all_to_all(tiles, axis, 0, 0, tiled=True)
    return jnp.sum(tiles.astype(jnp.float32), axis=0)


def local(port_vectors, column_leaf, transfer, row_leaf):
    bit_count = lax.axis_size("bfly").bit_length() - 1
    state = jnp.dot(
        column_leaf[0, 0], port_vectors[0, 0], preferred_element_type=jnp.float32
    ).astype(jnp.bfloat16)
    for level in range(transfer.shape[1]):
        stacked = with_partner(state, "bfly", level % bit_count)
        state = jnp.dot(
            transfer[0, level, 0], stacked, preferred_element_type=jnp.float32
        ).astype(jnp.bfloat16)
    partial_rows = jnp.dot(row_leaf[0, 0], state, preferred_element_type=jnp.float32)
    summed = sent_and_summed(partial_rows.astype(jnp.bfloat16), "blk")
    scaled = summed * (1.0 / math.sqrt(lax.axis_size("blk")))
    return scaled.astype(jnp.bfloat16)[None]


def solution(mesh):
    placed = (
        P("blk", "bfly", None, None),
        P("blk", "bfly", None, None),
        P("blk", None, "bfly", None, None),
        P("blk", "bfly", None, None),
    )
    return jax.shard_map(
        local, mesh=mesh, in_specs=placed, out_specs=P("bfly", "blk", None), check_vma=False
    )
```

time: 72.9 us -> 59.9 us (0.82)
  starting transfers between devices: 15 us -> 0 us
  blocking collectives: 41.2 us -> 54.6 us
  waiting for transfers between devices: 10 us -> 0 us
  local copies, waits for them, and re-layouts: 1.92 us -> 0.17 us
    all_gather x0 -> x4, blocking collectives: none -> 21 us  [with_partner(): return lax.all_gather(array, axis, axis_index_groups=pairs, tiled=True)]
    ppermute x4 -> x0, starting transfers between devices: 15 us -> none  [from_partner(): lax.ppermute(array, axis, [(i, i ^ 1 << bit) for i in range(lax.axis_size...]
    ppermute x4 -> x0, waiting for transfers between devices: 10 us -> none  [from_partner(): lax.ppermute(array, axis, [(i, i ^ 1 << bit) for i in range(lax.axis_size...]
    all_to_all x1, blocking collectives: 41.2 us -> 33.5 us  [sent_and_summed(): tiles = lax.all_to_all(tiles, axis, 0, 0, tiled=True)]
    squeeze x1 -> x0, local copies, waits for them, and re-layouts: 1.76 us -> none  [local(): matrix = transfer[0, level, 0]]
    dot_general x8 -> x4, matrix products: 2.2 us -> 2.63 us  [the longest x3 2.01 us: local(): jnp.dot(transfer[0, level, 0], stacked, preferred_element_type=jnp.float32)]
  transfers between devices with their start and end apart: 4 -> 0, of which waited for: 3 -> 0; matrix products, arithmetic and copies ran while one was open for 2% -> 0% of each run, Pallas kernels for 0% -> 0%
where the time goes in v1:
time: 59.9 us; the launch traced here: 59.6 us
  blocking collectives  54.6 us (91%)
  matrix products  4.2 us (7%)
  other arithmetic  0.64 us (1%)
    all_to_all x1, blocking collectives, sent_and_summed(): tiles = lax.all_to_all(tiles, axis, 0, 0, tiled=True)  33.5 us
    all_gather x4, blocking collectives, with_partner(): return lax.all_gather(array, axis, axis_index_groups=pairs, tiled=True)  21 us
    dot_general x3, matrix products, local(): jnp.dot(transfer[0, level, 0], stacked, preferred_element_type=jnp.float32)  2.01 us
    dot_general x1, matrix products, local(): jnp.dot(column_leaf[0, 0], port_vectors[0, 0], preferred_element_type=jnp...  1.57 us

profile of v1, /device:TPU:24, one launch (start us, length us, event | category | flops | bytes accessed | tf_op | source)
XLA Modules:
  0.0 59.6 jit_solution(12934724627041705283)
XLA Ops:
  0.0 0.0 copy-start
  0.0 0.0 copy-start.1
  0.0 1.6 %convolution_convert_fusion.5 = bf16[384,128]{1,0:T(8,128)(2,1)S(1)} fusion(bf16[1,1,384,768]{3,2,1,0:T(8,128)(2,1)} %param.5, bf16[1,1,768,128]{3,2,1,0:T(8,128)(2,1)} %param.4), kind=kOutput, calls=%fused_computation.6 | convolution fusion | flops 75546624 | bytes 884736 | tf_op jit(solution)/shard_map/dot_general | solution.py:23
  1.6 1.9 %all_gather.12 = bf16[768,128]{1,0:T(8,128)(2,1)S(1)} all-gather(bf16[384,128]{1,0:T(8,128)(2,1)S(1)} %convolution_convert_fusion.5), channel_id=1, replica_groups={{0,1},{2,3},{4,5},{6,7},{8,9},{10,11},{12,13},{14,15},{16,17},{18,19},{..., dimensions={0}, use_global_device_ids=true | all-gather | bytes 294912 | tf_op jit(solution)/shard_map/all_gather | solution.py:11
  3.5 1.4 %fusion.1 = bf16[384,128]{0,1:T(8,128)(2,1)S(1)} fusion(bf16[768,128]{1,0:T(8,128)(2,1)S(1)} %all_gather.12, bf16[1,4,1,384,768]{4,3,2,1,0:T(8,128)(2,1)} %param.6), kind=kOutput, calls=%fused_computation.7 | convolution fusion | flops 75546624 | bytes 884736 | tf_op jit(solution)/shard_map/dot_general | solution.py:28
  4.9 5.5 %all_gather.13 = bf16[768,128]{0,1:T(8,128)(2,1)S(1)} all-gather(bf16[384,128]{0,1:T(8,128)(2,1)S(1)} %fusion.1), channel_id=1, replica_groups={{0,2},{1,3},{4,6},{5,7},{8,10},{9,11},{12,14},{13,15},{16,18},{17,19},{..., dimensions={0}, use_global_device_ids=true | all-gather | bytes 294912 | tf_op jit(solution)/shard_map/all_gather | solution.py:11
  10.5 0.0 copy-done.1
  10.5 0.3 fusion.2
  10.8 5.3 %all_gather.14 = bf16[768,128]{0,1:T(8,128)(2,1)S(1)} all-gather(bf16[384,128]{0,1:T(8,128)(2,1)S(1)} %fusion.2), channel_id=1, replica_groups={{0,4},{1,5},{2,6},{3,7},{8,12},{9,13},{10,14},{11,15},{16,20},{17,21},{..., dimensions={0}, use_global_device_ids=true | all-gather | bytes 294912 | tf_op jit(solution)/shard_map/all_gather | solution.py:11
  16.1 0.3 fusion.3
  16.4 8.3 %all_gather.15 = bf16[768,128]{0,1:T(8,128)(2,1)S(1)} all-gather(bf16[384,128]{0,1:T(8,128)(2,1)S(1)} %fusion.3), channel_id=1, replica_groups={{0,8},{1,9},{2,10},{3,11},{4,12},{5,13},{6,14},{7,15},{16,24},{17,25},{..., dimensions={0}, use_global_device_ids=true | all-gather | bytes 294912 | tf_op jit(solution)/shard_map/all_gather | solution.py:11
  24.7 0.0 copy-done
  24.7 0.6 %fusion = bf16[768,128]{0,1:T(8,128)(2,1)S(1)} fusion(bf16[768,128]{0,1:T(8,128)(2,1)S(1)} %all_gather.15, bf16[1,1,768,384]{3,2,1,0:T(8,128)(2,1)S(1)} %copy-done, bf16[1,4,1,384,768]{4,3,2,1,0:T(8,128)(2,1)S(1)} %copy-done.1), kind=kOutput, calls=%fused_computation.1 | convolution fusion | flops 151142400 | bytes 1572864 | tf_op jit(solution)/shard_map/dot_general | solution.py:31
  25.3 0.2 copy.5
  25.5 33.5 %all_to_all.5 = bf16[32,24,128]{2,1,0:T(8,128)(2,1)S(1)} all-to-all(bf16[32,24,128]{2,1,0:T(8,128)(2,1)S(1)} %bitcast.37), channel_id=1, replica_groups=mesh['blk'=32,'bfly'=16] {'blk'}, dimensions={0} | all-to-all | bytes 393216 | tf_op jit(solution)/shard_map/all_to_all | solution.py:17
  59.0 0.6 %fusion.17 = bf16[1,24,128]{2,1,0:T(8,128)(2,1)} fusion(f32[24,128]{1,0:T(8,128)S(1)} %convert_reduce_fusion), kind=kLoop, calls=%fused_computation.23 | loop fusion | flops 6144 | bytes 18432 | tf_op jit(solution)/shard_map/convert_element_type | solution.py:34
  (1 shorter events, 0.0 us)
Async XLA Ops:
  0.0 24.7 %copy-start = (bf16[1,1,768,384]{3,2,1,0:T(8,128)(2,1)S(1)}, bf16[1,1,768,384]{3,2,1,0:T(8,128)(2,1)}, u32[]{:S(2)}) copy-start(bf16[1,1,768,384]{3,2,1,0:T(8,128)(2,1)} %param.7) | copy-start | bytes 1769476
  0.0 10.5 %copy-start.1 = (bf16[1,4,1,384,768]{4,3,2,1,0:T(8,128)(2,1)S(1)}, bf16[1,4,1,384,768]{4,3,2,1,0:T(8,128)(2,1)}, u32[]{:S(2)}) copy-start(bf16[1,4,1,384,768]{4,3,2,1,0:T(8,128)(2,1)} %param.6) | copy-start | bytes 7077892

commit v2 on v1

v2 whole, which is shorter than its diff:
```python
import functools
import math

import jax
import jax.numpy as jnp
from jax import lax
from jax.experimental import pallas as pl
from jax.experimental.pallas import tpu as pltpu
from jax.sharding import PartitionSpec as P

VMEM = pl.BlockSpec(memory_space=pltpu.VMEM)


def rows_kernel(shift, state, leaf, out):
    rows = leaf.shape[2]
    product = jnp.dot(leaf[0, 0], state[...], preferred_element_type=jnp.float32)
    product = product.astype(out.dtype)
    out[: rows - shift] = product[shift:]
    out[rows - shift :] = product[:shift]


def partial_rows(state, leaf, shift):
    return pl.pallas_call(
        functools.partial(rows_kernel, shift),
        out_shape=jax.ShapeDtypeStruct((leaf.shape[2], state.shape[1]), jnp.bfloat16),
        in_specs=[VMEM, VMEM],
        out_specs=VMEM,
        compiler_params=pltpu.CompilerParams(vmem_limit_bytes=8 << 20),
        name="partial_rows",
    )(state, leaf)


def with_partner(array, axis, bit):
    pairs = [[i, i | 1 << bit] for i in range(lax.axis_size(axis)) if not i >> bit & 1]
    return lax.all_gather(array, axis, axis_index_groups=pairs, tiled=True)


def local(port_vectors, column_leaf, transfer, row_leaf):
    bit_count = lax.axis_size("bfly").bit_length() - 1
    count = lax.axis_size("blk")
    state = jnp.dot(
        column_leaf[0, 0], port_vectors[0, 0], preferred_element_type=jnp.float32
    ).astype(jnp.bfloat16)
    for level in range(transfer.shape[1]):
        stacked = with_partner(state, "bfly", level % bit_count)
        state = jnp.dot(
            transfer[0, level, 0], stacked, preferred_element_type=jnp.float32
        ).astype(jnp.bfloat16)
    start = count // 2
    order = [(i + start) % count for i in range(count)]
    owned = row_leaf.shape[2] // count
    tiles = partial_rows(state, row_leaf, start * owned).reshape(count, owned, -1)
    tiles = lax.all_to_all(tiles, "blk", 0, 0, axis_index_groups=[order], tiled=True)
    summed = jnp.sum(tiles.astype(jnp.float32), axis=0)
    return (summed * (1.0 / math.sqrt(count))).astype(jnp.bfloat16)[None]


def solution(mesh):
    placed = (
        P("blk", "bfly", None, None),
        P("blk", "bfly", None, None),
        P("blk", None, "bfly", None, None),
        P("blk", "bfly", None, None),
    )
    return jax.shard_map(
        local, mesh=mesh, in_specs=placed, out_specs=P("bfly", "blk", None), check_vma=False
    )
```

time: 59.9 us -> 55.4 us (0.925)
  blocking collectives: 54.6 us -> 49.4 us
  local copies, waits for them, and re-layouts: 0.17 us -> 1.07 us
    all_to_all x1, blocking collectives: 33.5 us -> 28.4 us  [local(): lax.all_to_all(tiles, 'blk', 0, 0, axis_index_groups=[order], tiled=True)]
    unnamed x4 -> x6, local copies, waits for them, and re-layouts: 0.01 us -> 1.07 us
    dot_general x1 -> x0, matrix products: 0.62 us -> none  [local(): jnp.dot(row_leaf[0, 0], state, preferred_element_type=jnp.float32)]
    dot_general x3 -> x4, matrix products: 2.01 us -> 2.38 us  [local(): jnp.dot(transfer[0, level, 0], stacked, preferred_element_type=jnp.float32)]
where the time goes in v2:
time: 55.4 us; the launch traced here: 55.1 us
  blocking collectives  49.4 us (89%)
  matrix products  3.62 us (7%)
  local copies, waits for them, and re-layouts  1.07 us (2%)
  other arithmetic  0.64 us (1%)
    all_to_all x1, blocking collectives, local(): lax.all_to_all(tiles, 'blk', 0, 0, axis_index_groups=[order], tiled=True)  28.4 us
    all_gather x4, blocking collectives, with_partner(): return lax.all_gather(array, axis, axis_index_groups=pairs, tiled=True)  21 us
    dot_general x4, matrix products, local(): jnp.dot(transfer[0, level, 0], stacked, preferred_element_type=jnp.float32)  2.38 us
    dot_general x1, matrix products, local(): jnp.dot(column_leaf[0, 0], port_vectors[0, 0], preferred_element_type=jnp...  1.24 us

profile of v2, /device:TPU:24, one launch (start us, length us, event | category | flops | bytes accessed | tf_op | source)
XLA Modules:
  0.0 55.1 jit_solution(12319512484618595506)
XLA Ops:
  0.0 0.0 copy-start
  0.0 0.0 copy-start.2
  0.0 1.1 %copy-done = bf16[1,1,384,768]{3,2,1,0:T(8,128)(2,1)S(1)} copy-done((bf16[1,1,384,768]{3,2,1,0:T(8,128)(2,1)S(1)}, bf16[1,1,384,768]{3,2,1,0:T(8,128)(2,1)}, u32[]{:S(2)}) %copy-start) | copy-done | bytes 589848
  1.1 1.2 %convolution_convert_fusion.4 = bf16[384,128]{1,0:T(8,128)(2,1)S(1)} fusion(bf16[1,1,384,768]{3,2,1,0:T(8,128)(2,1)S(1)} %copy-done, bf16[1,1,768,128]{3,2,1,0:T(8,128)(2,1)} %param.4), kind=kOutput, calls=%fused_computation.4 | convolution fusion | flops 75546624 | bytes 884736 | tf_op jit(solution)/shard_map/dot_general | solution.py:41
  2.3 1.9 %all_gather.12 = bf16[768,128]{1,0:T(8,128)(2,1)S(1)} all-gather(bf16[384,128]{1,0:T(8,128)(2,1)S(1)} %convolution_convert_fusion.4), channel_id=1, replica_groups={{0,1},{2,3},{4,5},{6,7},{8,9},{10,11},{12,13},{14,15},{16,17},{18,19},{..., dimensions={0}, use_global_device_ids=true | all-gather | bytes 294912 | tf_op jit(solution)/shard_map/all_gather | solution.py:35
  4.3 0.0 copy-start.1
  4.3 1.4 %fusion = bf16[384,128]{0,1:T(8,128)(2,1)S(1)} fusion(bf16[768,128]{1,0:T(8,128)(2,1)S(1)} %all_gather.12, bf16[1,4,1,384,768]{4,3,2,1,0:T(8,128)(2,1)} %param.6), kind=kOutput, calls=%fused_computation.5 | convolution fusion | flops 75546624 | bytes 884736 | tf_op jit(solution)/shard_map/dot_general | solution.py:46
  5.7 5.5 %all_gather.13 = bf16[768,128]{0,1:T(8,128)(2,1)S(1)} all-gather(bf16[384,128]{0,1:T(8,128)(2,1)S(1)} %fusion), channel_id=1, replica_groups={{0,2},{1,3},{4,6},{5,7},{8,10},{9,11},{12,14},{13,15},{16,18},{17,19},{..., dimensions={0}, use_global_device_ids=true | all-gather | bytes 294912 | tf_op jit(solution)/shard_map/all_gather | solution.py:35
  11.2 0.0 copy-done.2
  11.3 0.3 fusion.1
  11.6 5.3 %all_gather.14 = bf16[768,128]{0,1:T(8,128)(2,1)S(1)} all-gather(bf16[384,128]{0,1:T(8,128)(2,1)S(1)} %fusion.1), channel_id=1, replica_groups={{0,4},{1,5},{2,6},{3,7},{8,12},{9,13},{10,14},{11,15},{16,20},{17,21},{..., dimensions={0}, use_global_device_ids=true | all-gather | bytes 294912 | tf_op jit(solution)/shard_map/all_gather | solution.py:35
  16.9 0.3 fusion.2
  17.2 8.3 %all_gather.15 = bf16[768,128]{0,1:T(8,128)(2,1)S(1)} all-gather(bf16[384,128]{0,1:T(8,128)(2,1)S(1)} %fusion.2), channel_id=1, replica_groups={{0,8},{1,9},{2,10},{3,11},{4,12},{5,13},{6,14},{7,15},{16,24},{17,25},{..., dimensions={0}, use_global_device_ids=true | all-gather | bytes 294912 | tf_op jit(solution)/shard_map/all_gather | solution.py:35
  25.5 0.3 fusion.3.state
  25.8 0.0 copy-done.1
  25.8 0.3 partial_rows.1
  26.1 28.4 %all_to_all.5 = bf16[32,24,128]{2,1,0:T(8,128)(2,1)S(1)} all-to-all(bf16[32,24,128]{2,1,0:T(8,128)(2,1)S(1)} %bitcast.33), channel_id=1, replica_groups={{256,272,288,304,320,336,352,368,384,400,416,432,448,464,480,496,0,16,3..., dimensions={0} | all-to-all | bytes 393216 | tf_op jit(solution)/shard_map/all_to_all | solution.py:53
  54.5 0.6 %fusion.14 = bf16[1,24,128]{2,1,0:T(8,128)(2,1)} fusion(f32[24,128]{1,0:T(8,128)S(1)} %convert_reduce_fusion), kind=kLoop, calls=%fused_computation.21 | loop fusion | flops 6144 | bytes 18432 | tf_op jit(solution)/shard_map/convert_element_type | solution.py:55
  (1 shorter events, 0.0 us)
Async XLA Ops:
  0.0 1.1 %copy-start = (bf16[1,1,384,768]{3,2,1,0:T(8,128)(2,1)S(1)}, bf16[1,1,384,768]{3,2,1,0:T(8,128)(2,1)}, u32[]{:S(2)}) copy-start(bf16[1,1,384,768]{3,2,1,0:T(8,128)(2,1)} %param.5) | copy-start | bytes 1769476
  0.0 11.2 %copy-start.2 = (bf16[1,4,1,384,768]{4,3,2,1,0:T(8,128)(2,1)S(1)}, bf16[1,4,1,384,768]{4,3,2,1,0:T(8,128)(2,1)}, u32[]{:S(2)}) copy-start(bf16[1,4,1,384,768]{4,3,2,1,0:T(8,128)(2,1)} %param.6) | copy-start | bytes 7077892
  4.3 21.5 %copy-start.1 = (bf16[1,1,768,384]{3,2,1,0:T(8,128)(2,1)S(1)}, bf16[1,1,768,384]{3,2,1,0:T(8,128)(2,1)}, u32[]{:S(2)}) copy-start(bf16[1,1,768,384]{3,2,1,0:T(8,128)(2,1)} %leaf.1) | copy-start | bytes 1769476

commit v3 on v2

--- a/solution.py
+++ b/solution.py
@@ -9,6 +9,46 @@
 from jax.sharding import PartitionSpec as P
 
 VMEM = pl.BlockSpec(memory_space=pltpu.VMEM)
+HBM = pl.BlockSpec(memory_space=pltpu.HBM)
+
+
+def leaf_kernel(ports, leaf, transfer, state, first, ports_v, leaf_v, sems):
+    copies = [
+        pltpu.make_async_copy(leaf.at[0, 0], leaf_v, sems.at[0]),
+        pltpu.make_async_copy(ports.at[0, 0], ports_v, sems.at[1]),
+        pltpu.make_async_copy(transfer.at[0, 0, 0], first, sems.at[2]),
+    ]
+    for copy in copies:
+        copy.start()
+    copies[0].wait()
+    copies[1].wait()
+    state[...] = jnp.dot(
+        leaf_v[...], ports_v[...], preferred_element_type=jnp.float32
+    ).astype(state.dtype)
+    copies[2].wait()
+
+
+def leaf_state(ports, leaf, transfer):
+    rank = leaf.shape[2]
+    held = [
+        pltpu.with_memory_space_constraint(x, pltpu.HBM) for x in (ports, leaf, transfer)
+    ]
+    return pl.pallas_call(
+        leaf_kernel,
+        out_shape=(
+            jax.ShapeDtypeStruct((rank, ports.shape[3]), jnp.bfloat16),
+            jax.ShapeDtypeStruct(transfer.shape[3:], jnp.bfloat16),
+        ),
+        in_specs=[HBM] * 3,
+        out_specs=(VMEM, VMEM),
+        scratch_shapes=[
+            pltpu.VMEM(ports.shape[2:], jnp.bfloat16),
+            pltpu.VMEM(leaf.shape[2:], jnp.bfloat16),
+            pltpu.SemaphoreType.DMA((3,)),
+        ],
+        compiler_params=pltpu.CompilerParams(vmem_limit_bytes=8 << 20),
+        name="leaf_state",
+    )(*held)
 
 
 def rows_kernel(shift, state, leaf, out):
@@ -38,14 +78,13 @@
 def local(port_vectors, column_leaf, transfer, row_leaf):
     bit_count = lax.axis_size("bfly").bit_length() - 1
     count = lax.axis_size("blk")
-    state = jnp.dot(
-        column_leaf[0, 0], port_vectors[0, 0], preferred_element_type=jnp.float32
-    ).astype(jnp.bfloat16)
+    state, first = leaf_state(port_vectors, column_leaf, transfer)
+    state, transfer, row_leaf = lax.optimization_barrier((state, transfer, row_leaf))
     for level in range(transfer.shape[1]):
         stacked = with_partner(state, "bfly", level % bit_count)
-        state = jnp.dot(
-            transfer[0, level, 0], stacked, preferred_element_type=jnp.float32
-        ).astype(jnp.bfloat16)
+        matrix = transfer[0, level, 0] if level else first
+        state = jnp.dot(matrix, stacked, preferred_element_type=jnp.float32)
+        state = state.astype(jnp.bfloat16)
     start = count // 2
     order = [(i + start) % count for i in range(count)]
     owned = row_leaf.shape[2] // count

time: 55.4 us -> 53.5 us (0.966)
  matrix products: 3.62 us -> 1.26 us
  Pallas kernels: 0.32 us -> 1.91 us
  local copies, waits for them, and re-layouts: 1.07 us -> 0.01 us
    dot_general x5 -> x4, matrix products: 3.62 us -> 1.26 us  [local(): state = jnp.dot(matrix, stacked, preferred_element_type=jnp.float32)]
    pallas_call x0 -> x1, Pallas kernels: none -> 1.6 us  [leaf_state(): pl.pallas_call(leaf_kernel, out_shape=(jax.ShapeDtypeStruct((rank, ports....]
    unnamed x6 -> x4, local copies, waits for them, and re-layouts: 1.07 us -> 0.01 us
where the time goes in v3:
time: 53.5 us; the launch traced here: 53.3 us
  blocking collectives  49.4 us (92%)
  Pallas kernels  1.91 us (4%)
  matrix products  1.26 us (2%)
  other arithmetic  0.64 us (1%)
    all_to_all x1, blocking collectives, local(): lax.all_to_all(tiles, 'blk', 0, 0, axis_index_groups=[order], tiled=True)  28.4 us
    all_gather x4, blocking collectives, with_partner(): return lax.all_gather(array, axis, axis_index_groups=pairs, tiled=True)  21 us
    pallas_call x1, Pallas kernels, leaf_state(): pl.pallas_call(leaf_kernel, out_shape=(jax.ShapeDtypeStruct((rank, ports....  1.6 us
    dot_general x4, matrix products, local(): state = jnp.dot(matrix, stacked, preferred_element_type=jnp.float32)  1.26 us

profile of v3, /device:TPU:24, one launch (start us, length us, event | category | flops | bytes accessed | tf_op | source)
XLA Modules:
  0.0 53.3 jit_solution(11509335150834774202)
XLA Ops:
  0.0 0.0 copy-start.1
  0.0 1.6 %leaf_state.1 = (bf16[384,128]{1,0:T(8,128)(2,1)S(1)}, bf16[384,768]{1,0:T(8,128)(2,1)S(1)}) custom-call(bf16[1,1,768,128]{3,2,1,0:T(8,128)(2,1)} %ports.1, bf16[1,1,384,768]{3,2,1,0:T(8,128)(2,1)} %leaf.1, bf16[1,4,1,384,768]{4,3,2,1,0:T(8,128)(2,1)} %transfer.1), custom_call_target="tpu_custom_call" | custom-call | tf_op jit(solution)/shard_map/leaf_state/pallas_call | solution.py:36
  1.6 1.9 %all_gather.12 = bf16[768,128]{1,0:T(8,128)(2,1)S(1)} all-gather(bf16[384,128]{1,0:T(8,128)(2,1)S(1)} %get-tuple-element.13), channel_id=1, replica_groups={{0,1},{2,3},{4,5},{6,7},{8,9},{10,11},{12,13},{14,15},{16,17},{18,19},{..., dimensions={0}, use_global_device_ids=true | all-gather | bytes 294912 | tf_op jit(solution)/shard_map/all_gather | solution.py:75
  3.6 0.0 copy-start
  3.6 0.3 convolution_convert_fusion.3
  3.9 5.5 %all_gather.13 = bf16[768,128]{1,0:T(8,128)(2,1)S(1)} all-gather(bf16[384,128]{1,0:T(8,128)(2,1)S(1)} %convolution_convert_fusion.3), channel_id=1, replica_groups={{0,2},{1,3},{4,6},{5,7},{8,10},{9,11},{12,14},{13,15},{16,18},{17,19},{..., dimensions={0}, use_global_device_ids=true | all-gather | bytes 294912 | tf_op jit(solution)/shard_map/all_gather | solution.py:75
  9.4 0.0 copy-done.1
  9.4 0.3 convolution_convert_fusion.2
  9.7 5.3 %all_gather.14 = bf16[768,128]{1,0:T(8,128)(2,1)S(1)} all-gather(bf16[384,128]{1,0:T(8,128)(2,1)S(1)} %convolution_convert_fusion.2), channel_id=1, replica_groups={{0,4},{1,5},{2,6},{3,7},{8,12},{9,13},{10,14},{11,15},{16,20},{17,21},{..., dimensions={0}, use_global_device_ids=true | all-gather | bytes 294912 | tf_op jit(solution)/shard_map/all_gather | solution.py:75
  15.0 0.3 convolution_convert_fusion.1
  15.4 8.3 %all_gather.15 = bf16[768,128]{1,0:T(8,128)(2,1)S(1)} all-gather(bf16[384,128]{1,0:T(8,128)(2,1)S(1)} %convolution_convert_fusion.1), channel_id=1, replica_groups={{0,8},{1,9},{2,10},{3,11},{4,12},{5,13},{6,14},{7,15},{16,24},{17,25},{..., dimensions={0}, use_global_device_ids=true | all-gather | bytes 294912 | tf_op jit(solution)/shard_map/all_gather | solution.py:75
  23.6 0.3 convolution_convert_fusion.state
  23.9 0.0 copy-done
  24.0 0.3 partial_rows.1
  24.3 28.4 %all_to_all.5 = bf16[32,24,128]{2,1,0:T(8,128)(2,1)S(1)} all-to-all(bf16[32,24,128]{2,1,0:T(8,128)(2,1)S(1)} %bitcast.17), channel_id=1, replica_groups={{256,272,288,304,320,336,352,368,384,400,416,432,448,464,480,496,0,16,3..., dimensions={0} | all-to-all | bytes 393216 | tf_op jit(solution)/shard_map/all_to_all | solution.py:92
  52.7 0.6 %fusion.6 = bf16[1,24,128]{2,1,0:T(8,128)(2,1)} fusion(f32[24,128]{1,0:T(8,128)S(1)} %convert_reduce_fusion), kind=kLoop, calls=%fused_computation.12 | loop fusion | flops 6144 | bytes 18432 | tf_op jit(solution)/shard_map/convert_element_type | solution.py:94
  (1 shorter events, 0.0 us)
Async XLA Ops:
  0.0 9.4 %copy-start.1 = (bf16[1,4,1,384,768]{4,3,2,1,0:T(8,128)(2,1)S(1)}, bf16[1,4,1,384,768]{4,3,2,1,0:T(8,128)(2,1)}, u32[]{:S(2)}) copy-start(bf16[1,4,1,384,768]{4,3,2,1,0:T(8,128)(2,1)} %transfer.1) | copy-start | bytes 7077892
  3.6 20.4 %copy-start = (bf16[1,1,768,384]{3,2,1,0:T(8,128)(2,1)S(1)}, bf16[1,1,768,384]{3,2,1,0:T(8,128)(2,1)}, u32[]{:S(2)}) copy-start(bf16[1,1,768,384]{3,2,1,0:T(8,128)(2,1)} %leaf.2) | copy-start | bytes 1769476

commit v4 on v3

--- a/solution.py
+++ b/solution.py
@@ -85,7 +85,7 @@
         matrix = transfer[0, level, 0] if level else first
         state = jnp.dot(matrix, stacked, preferred_element_type=jnp.float32)
         state = state.astype(jnp.bfloat16)
-    start = count // 2
+    start = count * 5 // 8
     order = [(i + start) % count for i in range(count)]
     owned = row_leaf.shape[2] // count
     tiles = partial_rows(state, row_leaf, start * owned).reshape(count, owned, -1)

time: 53.5 us -> 53.2 us (level)
  no operation moved by 1% of the time
where the time goes in v4:
time: 53.2 us; the launch traced here: 53 us
  blocking collectives  49.1 us (92%)
  Pallas kernels  1.91 us (4%)
  matrix products  1.26 us (2%)
  other arithmetic  0.64 us (1%)
    all_to_all x1, blocking collectives, local(): lax.all_to_all(tiles, 'blk', 0, 0, axis_index_groups=[order], tiled=True)  28.1 us
    all_gather x4, blocking collectives, with_partner(): return lax.all_gather(array, axis, axis_index_groups=pairs, tiled=True)  21 us
    pallas_call x1, Pallas kernels, leaf_state(): pl.pallas_call(leaf_kernel, out_shape=(jax.ShapeDtypeStruct((rank, ports....  1.6 us
    dot_general x4, matrix products, local(): state = jnp.dot(matrix, stacked, preferred_element_type=jnp.float32)  1.26 us

profile of v4, /device:TPU:24, one launch (start us, length us, event | category | flops | bytes accessed | tf_op | source)
XLA Modules:
  0.0 53.0 jit_solution(9078938261322289226)
XLA Ops:
  0.0 0.0 copy-start.1
  0.0 1.6 %leaf_state.1 = (bf16[384,128]{1,0:T(8,128)(2,1)S(1)}, bf16[384,768]{1,0:T(8,128)(2,1)S(1)}) custom-call(bf16[1,1,768,128]{3,2,1,0:T(8,128)(2,1)} %ports.1, bf16[1,1,384,768]{3,2,1,0:T(8,128)(2,1)} %leaf.1, bf16[1,4,1,384,768]{4,3,2,1,0:T(8,128)(2,1)} %transfer.1), custom_call_target="tpu_custom_call" | custom-call | tf_op jit(solution)/shard_map/leaf_state/pallas_call | solution.py:36
  1.6 1.9 %all_gather.12 = bf16[768,128]{1,0:T(8,128)(2,1)S(1)} all-gather(bf16[384,128]{1,0:T(8,128)(2,1)S(1)} %get-tuple-element.13), channel_id=1, replica_groups={{0,1},{2,3},{4,5},{6,7},{8,9},{10,11},{12,13},{14,15},{16,17},{18,19},{..., dimensions={0}, use_global_device_ids=true | all-gather | bytes 294912 | tf_op jit(solution)/shard_map/all_gather | solution.py:75
  3.6 0.0 copy-start
  3.6 0.3 convolution_convert_fusion.3
  3.9 5.5 %all_gather.13 = bf16[768,128]{1,0:T(8,128)(2,1)S(1)} all-gather(bf16[384,128]{1,0:T(8,128)(2,1)S(1)} %convolution_convert_fusion.3), channel_id=1, replica_groups={{0,2},{1,3},{4,6},{5,7},{8,10},{9,11},{12,14},{13,15},{16,18},{17,19},{..., dimensions={0}, use_global_device_ids=true | all-gather | bytes 294912 | tf_op jit(solution)/shard_map/all_gather | solution.py:75
  9.4 0.0 copy-done.1
  9.4 0.3 convolution_convert_fusion.2
  9.7 5.3 %all_gather.14 = bf16[768,128]{1,0:T(8,128)(2,1)S(1)} all-gather(bf16[384,128]{1,0:T(8,128)(2,1)S(1)} %convolution_convert_fusion.2), channel_id=1, replica_groups={{0,4},{1,5},{2,6},{3,7},{8,12},{9,13},{10,14},{11,15},{16,20},{17,21},{..., dimensions={0}, use_global_device_ids=true | all-gather | bytes 294912 | tf_op jit(solution)/shard_map/all_gather | solution.py:75
  15.0 0.3 convolution_convert_fusion.1
  15.4 8.3 %all_gather.15 = bf16[768,128]{1,0:T(8,128)(2,1)S(1)} all-gather(bf16[384,128]{1,0:T(8,128)(2,1)S(1)} %convolution_convert_fusion.1), channel_id=1, replica_groups={{0,8},{1,9},{2,10},{3,11},{4,12},{5,13},{6,14},{7,15},{16,24},{17,25},{..., dimensions={0}, use_global_device_ids=true | all-gather | bytes 294912 | tf_op jit(solution)/shard_map/all_gather | solution.py:75
  23.6 0.3 convolution_convert_fusion.state
  23.9 0.0 copy-done
  24.0 0.3 partial_rows.1
  24.3 28.1 %all_to_all.5 = bf16[32,24,128]{2,1,0:T(8,128)(2,1)S(1)} all-to-all(bf16[32,24,128]{2,1,0:T(8,128)(2,1)S(1)} %bitcast.17), channel_id=1, replica_groups={{320,336,352,368,384,400,416,432,448,464,480,496,0,16,32,48,64,80,96,11..., dimensions={0} | all-to-all | bytes 393216 | tf_op jit(solution)/shard_map/all_to_all | solution.py:92
  52.4 0.6 %fusion.6 = bf16[1,24,128]{2,1,0:T(8,128)(2,1)} fusion(f32[24,128]{1,0:T(8,128)S(1)} %convert_reduce_fusion), kind=kLoop, calls=%fused_computation.12 | loop fusion | flops 6144 | bytes 18432 | tf_op jit(solution)/shard_map/convert_element_type | solution.py:94
  (1 shorter events, 0.0 us)
Async XLA Ops:
  0.0 9.4 %copy-start.1 = (bf16[1,4,1,384,768]{4,3,2,1,0:T(8,128)(2,1)S(1)}, bf16[1,4,1,384,768]{4,3,2,1,0:T(8,128)(2,1)}, u32[]{:S(2)}) copy-start(bf16[1,4,1,384,768]{4,3,2,1,0:T(8,128)(2,1)} %transfer.1) | copy-start | bytes 7077892
  3.6 20.4 %copy-start = (bf16[1,1,768,384]{3,2,1,0:T(8,128)(2,1)S(1)}, bf16[1,1,768,384]{3,2,1,0:T(8,128)(2,1)}, u32[]{:S(2)}) copy-start(bf16[1,1,768,384]{3,2,1,0:T(8,128)(2,1)} %leaf.2) | copy-start | bytes 1769476

commit v5 on v4

--- a/solution.py
+++ b/solution.py
@@ -54,9 +54,8 @@
 def rows_kernel(shift, state, leaf, out):
     rows = leaf.shape[2]
     product = jnp.dot(leaf[0, 0], state[...], preferred_element_type=jnp.float32)
-    product = product.astype(out.dtype)
-    out[: rows - shift] = product[shift:]
-    out[rows - shift :] = product[:shift]
+    out[: rows - shift] = product[shift:].astype(out.dtype)
+    out[rows - shift :] = product[:shift].astype(out.dtype)
 
 
 def partial_rows(state, leaf, shift):
@@ -85,7 +84,7 @@
         matrix = transfer[0, level, 0] if level else first
         state = jnp.dot(matrix, stacked, preferred_element_type=jnp.float32)
         state = state.astype(jnp.bfloat16)
-    start = count * 5 // 8
+    start = count * 5 // 8 - 1
     order = [(i + start) % count for i in range(count)]
     owned = row_leaf.shape[2] // count
     tiles = partial_rows(state, row_leaf, start * owned).reshape(count, owned, -1)

time: 53.2 us -> 51.3 us (0.964)
  blocking collectives: 49.1 us -> 47.1 us
    all_to_all x1, blocking collectives: 28.1 us -> 26.1 us  [local(): lax.all_to_all(tiles, 'blk', 0, 0, axis_index_groups=[order], tiled=True)]
where the time goes in v5:
time: 51.3 us; the launch traced here: 51 us
  blocking collectives  47.1 us (92%)
  Pallas kernels  1.91 us (4%)
  matrix products  1.26 us (2%)
  other arithmetic  0.64 us (1%)
    all_to_all x1, blocking collectives, local(): lax.all_to_all(tiles, 'blk', 0, 0, axis_index_groups=[order], tiled=True)  26.1 us
    all_gather x4, blocking collectives, with_partner(): return lax.all_gather(array, axis, axis_index_groups=pairs, tiled=True)  21 us
    pallas_call x1, Pallas kernels, leaf_state(): pl.pallas_call(leaf_kernel, out_shape=(jax.ShapeDtypeStruct((rank, ports....  1.6 us
    dot_general x4, matrix products, local(): state = jnp.dot(matrix, stacked, preferred_element_type=jnp.float32)  1.26 us

profile of v5, /device:TPU:24, one launch (start us, length us, event | category | flops | bytes accessed | tf_op | source)
XLA Modules:
  0.0 51.0 jit_solution(5832382142694168609)
XLA Ops:
  0.0 0.0 copy-start.1
  0.0 1.6 %leaf_state.1 = (bf16[384,128]{1,0:T(8,128)(2,1)S(1)}, bf16[384,768]{1,0:T(8,128)(2,1)S(1)}) custom-call(bf16[1,1,768,128]{3,2,1,0:T(8,128)(2,1)} %ports.1, bf16[1,1,384,768]{3,2,1,0:T(8,128)(2,1)} %leaf.1, bf16[1,4,1,384,768]{4,3,2,1,0:T(8,128)(2,1)} %transfer.1), custom_call_target="tpu_custom_call" | custom-call | tf_op jit(solution)/shard_map/leaf_state/pallas_call | solution.py:36
  1.6 1.9 %all_gather.12 = bf16[768,128]{1,0:T(8,128)(2,1)S(1)} all-gather(bf16[384,128]{1,0:T(8,128)(2,1)S(1)} %get-tuple-element.13), channel_id=1, replica_groups={{0,1},{2,3},{4,5},{6,7},{8,9},{10,11},{12,13},{14,15},{16,17},{18,19},{..., dimensions={0}, use_global_device_ids=true | all-gather | bytes 294912 | tf_op jit(solution)/shard_map/all_gather | solution.py:74
  3.6 0.0 copy-start
  3.6 0.3 convolution_convert_fusion.3
  3.9 5.5 %all_gather.13 = bf16[768,128]{1,0:T(8,128)(2,1)S(1)} all-gather(bf16[384,128]{1,0:T(8,128)(2,1)S(1)} %convolution_convert_fusion.3), channel_id=1, replica_groups={{0,2},{1,3},{4,6},{5,7},{8,10},{9,11},{12,14},{13,15},{16,18},{17,19},{..., dimensions={0}, use_global_device_ids=true | all-gather | bytes 294912 | tf_op jit(solution)/shard_map/all_gather | solution.py:74
  9.4 0.0 copy-done.1
  9.4 0.3 convolution_convert_fusion.2
  9.7 5.3 %all_gather.14 = bf16[768,128]{1,0:T(8,128)(2,1)S(1)} all-gather(bf16[384,128]{1,0:T(8,128)(2,1)S(1)} %convolution_convert_fusion.2), channel_id=1, replica_groups={{0,4},{1,5},{2,6},{3,7},{8,12},{9,13},{10,14},{11,15},{16,20},{17,21},{..., dimensions={0}, use_global_device_ids=true | all-gather | bytes 294912 | tf_op jit(solution)/shard_map/all_gather | solution.py:74
  15.0 0.3 convolution_convert_fusion.1
  15.4 8.3 %all_gather.15 = bf16[768,128]{1,0:T(8,128)(2,1)S(1)} all-gather(bf16[384,128]{1,0:T(8,128)(2,1)S(1)} %convolution_convert_fusion.1), channel_id=1, replica_groups={{0,8},{1,9},{2,10},{3,11},{4,12},{5,13},{6,14},{7,15},{16,24},{17,25},{..., dimensions={0}, use_global_device_ids=true | all-gather | bytes 294912 | tf_op jit(solution)/shard_map/all_gather | solution.py:74
  23.6 0.3 convolution_convert_fusion.state
  23.9 0.0 copy-done
  24.0 0.3 partial_rows.1
  24.3 26.1 %all_to_all.5 = bf16[32,24,128]{2,1,0:T(8,128)(2,1)S(1)} all-to-all(bf16[32,24,128]{2,1,0:T(8,128)(2,1)S(1)} %bitcast.17), channel_id=1, replica_groups={{304,320,336,352,368,384,400,416,432,448,464,480,496,0,16,32,48,64,80,9..., dimensions={0} | all-to-all | bytes 393216 | tf_op jit(solution)/shard_map/all_to_all | solution.py:91
  50.4 0.6 %fusion.6 = bf16[1,24,128]{2,1,0:T(8,128)(2,1)} fusion(f32[24,128]{1,0:T(8,128)S(1)} %convert_reduce_fusion), kind=kLoop, calls=%fused_computation.12 | loop fusion | flops 6144 | bytes 18432 | tf_op jit(solution)/shard_map/convert_element_type | solution.py:93
  (1 shorter events, 0.0 us)
Async XLA Ops:
  0.0 9.4 %copy-start.1 = (bf16[1,4,1,384,768]{4,3,2,1,0:T(8,128)(2,1)S(1)}, bf16[1,4,1,384,768]{4,3,2,1,0:T(8,128)(2,1)}, u32[]{:S(2)}) copy-start(bf16[1,4,1,384,768]{4,3,2,1,0:T(8,128)(2,1)} %transfer.1) | copy-start | bytes 7077892
  3.6 20.4 %copy-start = (bf16[1,1,768,384]{3,2,1,0:T(8,128)(2,1)S(1)}, bf16[1,1,768,384]{3,2,1,0:T(8,128)(2,1)}, u32[]{:S(2)}) copy-start(bf16[1,1,768,384]{3,2,1,0:T(8,128)(2,1)} %leaf.2) | copy-start | bytes 1769476

commit v6 on v5

--- a/solution.py
+++ b/solution.py
@@ -51,16 +51,17 @@
     )(*held)
 
 
-def rows_kernel(shift, state, leaf, out):
-    rows = leaf.shape[2]
+def rows_kernel(order, state, leaf, out):
+    owned = leaf.shape[2] // len(order)
     product = jnp.dot(leaf[0, 0], state[...], preferred_element_type=jnp.float32)
-    out[: rows - shift] = product[shift:].astype(out.dtype)
-    out[rows - shift :] = product[:shift].astype(out.dtype)
+    for i, block in enumerate(order):
+        rows = product[block * owned : (block + 1) * owned]
+        out[i * owned : (i + 1) * owned] = rows.astype(out.dtype)
 
 
-def partial_rows(state, leaf, shift):
+def partial_rows(state, leaf, order):
     return pl.pallas_call(
-        functools.partial(rows_kernel, shift),
+        functools.partial(rows_kernel, order),
         out_shape=jax.ShapeDtypeStruct((leaf.shape[2], state.shape[1]), jnp.bfloat16),
         in_specs=[VMEM, VMEM],
         out_specs=VMEM,
@@ -85,9 +86,9 @@
         state = jnp.dot(matrix, stacked, preferred_element_type=jnp.float32)
         state = state.astype(jnp.bfloat16)
     start = count * 5 // 8 - 1
-    order = [(i + start) % count for i in range(count)]
+    order = [(start - x + 14 * i) % count for x in (0, 1) for i in range(count // 2)]
     owned = row_leaf.shape[2] // count
-    tiles = partial_rows(state, row_leaf, start * owned).reshape(count, owned, -1)
+    tiles = partial_rows(state, row_leaf, order).reshape(count, owned, -1)
     tiles = lax.all_to_all(tiles, "blk", 0, 0, axis_index_groups=[order], tiled=True)
     summed = jnp.sum(tiles.astype(jnp.float32), axis=0)
     return (summed * (1.0 / math.sqrt(count))).astype(jnp.bfloat16)[None]

time: 51.3 us -> 51.1 us (level)
  no operation moved by 1% of the time
where the time goes in v6:
time: 51.1 us; the launch traced here: 50.9 us
  blocking collectives  47 us (92%)
  Pallas kernels  1.91 us (4%)
  matrix products  1.26 us (2%)
  other arithmetic  0.64 us (1%)
    all_to_all x1, blocking collectives, local(): lax.all_to_all(tiles, 'blk', 0, 0, axis_index_groups=[order], tiled=True)  26 us
    all_gather x4, blocking collectives, with_partner(): return lax.all_gather(array, axis, axis_index_groups=pairs, tiled=True)  21 us
    pallas_call x1, Pallas kernels, leaf_state(): pl.pallas_call(leaf_kernel, out_shape=(jax.ShapeDtypeStruct((rank, ports....  1.6 us
    dot_general x4, matrix products, local(): state = jnp.dot(matrix, stacked, preferred_element_type=jnp.float32)  1.26 us

profile of v6, /device:TPU:24, one launch (start us, length us, event | category | flops | bytes accessed | tf_op | source)
XLA Modules:
  0.0 50.9 jit_solution(18200194006206776613)
XLA Ops:
  0.0 0.0 copy-start.1
  0.0 1.6 %leaf_state.1 = (bf16[384,128]{1,0:T(8,128)(2,1)S(1)}, bf16[384,768]{1,0:T(8,128)(2,1)S(1)}) custom-call(bf16[1,1,768,128]{3,2,1,0:T(8,128)(2,1)} %ports.1, bf16[1,1,384,768]{3,2,1,0:T(8,128)(2,1)} %leaf.1, bf16[1,4,1,384,768]{4,3,2,1,0:T(8,128)(2,1)} %transfer.1), custom_call_target="tpu_custom_call" | custom-call | tf_op jit(solution)/shard_map/leaf_state/pallas_call | solution.py:36
  1.6 1.9 %all_gather.12 = bf16[768,128]{1,0:T(8,128)(2,1)S(1)} all-gather(bf16[384,128]{1,0:T(8,128)(2,1)S(1)} %get-tuple-element.13), channel_id=1, replica_groups={{0,1},{2,3},{4,5},{6,7},{8,9},{10,11},{12,13},{14,15},{16,17},{18,19},{..., dimensions={0}, use_global_device_ids=true | all-gather | bytes 294912 | tf_op jit(solution)/shard_map/all_gather | solution.py:75
  3.6 0.0 copy-start
  3.6 0.3 convolution_convert_fusion.3
  3.9 5.5 %all_gather.13 = bf16[768,128]{1,0:T(8,128)(2,1)S(1)} all-gather(bf16[384,128]{1,0:T(8,128)(2,1)S(1)} %convolution_convert_fusion.3), channel_id=1, replica_groups={{0,2},{1,3},{4,6},{5,7},{8,10},{9,11},{12,14},{13,15},{16,18},{17,19},{..., dimensions={0}, use_global_device_ids=true | all-gather | bytes 294912 | tf_op jit(solution)/shard_map/all_gather | solution.py:75
  9.4 0.0 copy-done.1
  9.4 0.3 convolution_convert_fusion.2
  9.7 5.3 %all_gather.14 = bf16[768,128]{1,0:T(8,128)(2,1)S(1)} all-gather(bf16[384,128]{1,0:T(8,128)(2,1)S(1)} %convolution_convert_fusion.2), channel_id=1, replica_groups={{0,4},{1,5},{2,6},{3,7},{8,12},{9,13},{10,14},{11,15},{16,20},{17,21},{..., dimensions={0}, use_global_device_ids=true | all-gather | bytes 294912 | tf_op jit(solution)/shard_map/all_gather | solution.py:75
  15.0 0.3 convolution_convert_fusion.1
  15.4 8.3 %all_gather.15 = bf16[768,128]{1,0:T(8,128)(2,1)S(1)} all-gather(bf16[384,128]{1,0:T(8,128)(2,1)S(1)} %convolution_convert_fusion.1), channel_id=1, replica_groups={{0,8},{1,9},{2,10},{3,11},{4,12},{5,13},{6,14},{7,15},{16,24},{17,25},{..., dimensions={0}, use_global_device_ids=true | all-gather | bytes 294912 | tf_op jit(solution)/shard_map/all_gather | solution.py:75
  23.6 0.3 convolution_convert_fusion.state
  23.9 0.0 copy-done
  24.0 0.3 partial_rows.1
  24.3 26.0 %all_to_all.5 = bf16[32,24,128]{2,1,0:T(8,128)(2,1)S(1)} all-to-all(bf16[32,24,128]{2,1,0:T(8,128)(2,1)S(1)} %bitcast.17), channel_id=1, replica_groups={{304,16,240,464,176,400,112,336,48,272,496,208,432,144,368,80,288,0,224..., dimensions={0} | all-to-all | bytes 393216 | tf_op jit(solution)/shard_map/all_to_all | solution.py:92
  50.3 0.6 %fusion.6 = bf16[1,24,128]{2,1,0:T(8,128)(2,1)} fusion(f32[24,128]{1,0:T(8,128)S(1)} %convert_reduce_fusion), kind=kLoop, calls=%fused_computation.12 | loop fusion | flops 6144 | bytes 18432 | tf_op jit(solution)/shard_map/convert_element_type | solution.py:94
  (1 shorter events, 0.0 us)
Async XLA Ops:
  0.0 9.4 %copy-start.1 = (bf16[1,4,1,384,768]{4,3,2,1,0:T(8,128)(2,1)S(1)}, bf16[1,4,1,384,768]{4,3,2,1,0:T(8,128)(2,1)}, u32[]{:S(2)}) copy-start(bf16[1,4,1,384,768]{4,3,2,1,0:T(8,128)(2,1)} %transfer.1) | copy-start | bytes 7077892
  3.6 20.4 %copy-start = (bf16[1,1,768,384]{3,2,1,0:T(8,128)(2,1)S(1)}, bf16[1,1,768,384]{3,2,1,0:T(8,128)(2,1)}, u32[]{:S(2)}) copy-start(bf16[1,1,768,384]{3,2,1,0:T(8,128)(2,1)} %leaf.2) | copy-start | bytes 1769476
